TPU v7x, 32 devices: a whole 2x2x4 slice. The times are simulated.
32 devices in a mesh: fsdp: 2 (over x), ctx: 4 (over y, core), tp: 4 (over z).
Axes of the slice: x: 2, y: 2, z: 4, core: 2. Of those that a mesh axis runs over, the one named last changes fastest.
Arguments:
- inputs: bfloat16 [8, 2048, 768], P('fsdp', ('ctx', 'tp')), may hold values from -6 to 6
- segments: int32 [8, 2048], P('fsdp'), may hold values from 0 to 15, never falling along the last dimension, each value on 1 to 1024 neighbouring positions
- query_weight: bfloat16 [768, 768], P(('fsdp', 'ctx'), 'tp'), may hold values from -0.3125 to 0.3125
- query_bias: float32 [768], P('tp'), may hold values from -1.5 to 1.5
- key_weight: bfloat16 [768, 768], P(('fsdp', 'ctx'), 'tp'), may hold values from -0.3125 to 0.3125
- value_weight: bfloat16 [768, 768], P(('fsdp', 'ctx'), 'tp'), may hold values from -0.21875 to 0.21875
- value_bias: float32 [768], P('tp'), may hold values from -1.5 to 1.5
- output_weight: bfloat16 [768, 768], P('tp', ('fsdp', 'ctx')), may hold values from -1.25 to 1.25
- output_bias: float32 [768], replicated, may hold values from -1.5 to 1.5
- first_gain: float32 [768], replicated, may hold values from 0.5 to 1.5
- first_shift: float32 [768], replicated, may hold values from -1.5 to 1.5
- expand_weight: bfloat16 [768, 3072], P(('fsdp', 'ctx'), 'tp'), may hold values from -0.21875 to 0.21875
- expand_bias: float32 [3072], P('tp'), may hold values from -1.5 to 1.5
- contract_weight: bfloat16 [3072, 768], P('tp', ('fsdp', 'ctx')), may hold values from -0.15625 to 0.15625
- contract_bias: float32 [768], replicated, may hold values from -1.5 to 1.5
- second_gain: float32 [768], replicated, may hold values from 0.5 to 1.5
- second_shift: float32 [768], replicated, may hold values from -1.5 to 1.5
- cotangent: bfloat16 [8, 2048, 768], P('fsdp', ('ctx', 'tp')), may hold values from -6 to 6
Outputs:
- outputs: bfloat16 [8, 2048, 768], P('fsdp', ('ctx', 'tp'))
- input_grad: bfloat16 [8, 2048, 768], P('fsdp', ('ctx', 'tp'))
- query_weight_grad: float32 [768, 768], P(('fsdp', 'ctx'), 'tp')
- query_bias_grad: float32 [768], P('tp')
- key_weight_grad: float32 [768, 768], P(('fsdp', 'ctx'), 'tp')
- value_weight_grad: float32 [768, 768], P(('fsdp', 'ctx'), 'tp')
- value_bias_grad: float32 [768], P('tp')
- output_weight_grad: float32 [768, 768], P('tp', ('fsdp', 'ctx'))
- output_bias_grad: float32 [768], replicated
- first_gain_grad: float32 [768], replicated
- first_shift_grad: float32 [768], replicated
- expand_weight_grad: float32 [768, 3072], P(('fsdp', 'ctx'), 'tp')
- expand_bias_grad: float32 [3072], P('tp')
- contract_weight_grad: float32 [3072, 768], P('tp', ('fsdp', 'ctx'))
- contract_bias_grad: float32 [768], replicated
- second_gain_grad: float32 [768], replicated
- second_shift_grad: float32 [768], replicated
Inputs may be any that keep to these rules, and one draw needn't show every extreme that they name: `segments`: along each sequence the segment numbers never fall and take every value 0 to 15; a document has at most 1024 tokens, and one document of each sequence has exactly 1024.
All inputs are finite; a program needn't handle non-finite values.
Results may differ from a plain program's by a relative error of at most 0.022.
Values may be sent and summed in bfloat16 or wider, within the bound.
No kernel may reach another device: no remote copies, remote signals or barrier semaphores. Data moves between devices by JAX's collectives and lax.ppermute only.
A program may use at most 192 MiB of HBM per device.

v0:
```python
import jax
import jax.numpy as jnp
from jax import lax
from jax.sharding import PartitionSpec as P

HEAD_DIM = 64
epsilon = 1e-05
masked_value = -1e30


def in_blocks(value, dim, count):
    lengths = value.shape
    tiles = value.reshape(*lengths[:dim], count, lengths[dim] // count, *lengths[dim + 1 :])
    return jnp.moveaxis(tiles, dim, 0)


def sent_and_summed(value, axis, dim):
    count = lax.axis_size(axis)
    tiles = lax.all_to_all(in_blocks(value, dim, count), axis, 0, 0, tiled=True)
    return jnp.sum(tiles.astype(jnp.float32), axis=0)


def in_one_piece(arrays, axis, dim, along):
    both = jnp.concatenate(arrays, axis=along)
    out, at, done = (sent_and_summed(both, axis, dim), 0, [])
    for a in arrays:
        done.append(lax.slice_in_dim(out, at, at + a.shape[along], axis=along))
        at += a.shape[along]
    return tuple(done)


def exact_gelu(values):
    return jax.nn.gelu(values, approximate=False)


def whole_rows(tensor):
    return lax.all_gather(tensor, "tp", axis=1, tiled=True)


def feature_sum(tensor):
    return lax.psum_scatter(
        tensor.astype(jnp.bfloat16), "tp", scatter_dimension=1, tiled=True
    ).astype(jnp.float32)


def fetch_weights(
    query_weight, key_weight, value_weight, expand_weight, output_weight, contract_weight
):
    front_set = (
        lax.all_gather(query_weight, ("fsdp", "ctx"), axis=0, tiled=True),
        lax.all_gather(key_weight, ("fsdp", "ctx"), axis=0, tiled=True),
        lax.all_gather(value_weight, ("fsdp", "ctx"), axis=0, tiled=True),
        lax.all_gather(expand_weight, ("fsdp", "ctx"), axis=0, tiled=True),
    )
    back_set = (
        lax.all_gather(output_weight, ("fsdp", "ctx"), axis=1, tiled=True),
        lax.all_gather(contract_weight, ("fsdp", "ctx"), axis=1, tiled=True),
    )
    return (front_set, back_set)


def fetch_blocks(keys_low, values_low):
    return (
        lax.all_gather(keys_low, "ctx", axis=1, tiled=True),
        lax.all_gather(values_low, "ctx", axis=1, tiled=True),
    )


def to_items(tensor):
    seq_count, row_count, feat_count = tensor.shape
    heads_here = feat_count // HEAD_DIM
    shaped = tensor.reshape(seq_count, row_count, heads_here, HEAD_DIM).transpose(0, 2, 1, 3)
    return shaped.reshape(seq_count * heads_here, row_count, HEAD_DIM)


def from_items(tensor, seq_count):
    item_count, row_count, _ = tensor.shape
    heads_here = item_count // seq_count
    shaped = tensor.reshape(seq_count, heads_here, row_count, HEAD_DIM).transpose(0, 2, 1, 3)
    return shaped.reshape(seq_count, row_count, heads_here * HEAD_DIM)


def masked_scores(query_rows, key_rows, query_segs, key_segs):
    raw_scores = lax.dot_general(
        query_rows, key_rows, (((1,), (1,)), ((), ())), preferred_element_type=jnp.float32
    ) * HEAD_DIM ** (-0.5)
    return jnp.where(query_segs[:, None] == key_segs[None, :], raw_scores, masked_value)


def attend(pieces):
    query_rows, key_rows, value_rows, query_segs, key_segs = pieces
    scores = masked_scores(query_rows, key_rows, query_segs, key_segs)
    highest = jnp.max(scores, axis=1, keepdims=True)
    weights = jnp.exp(scores - highest)
    totals = jnp.sum(weights, axis=1, keepdims=True)
    softmax_rows = (weights / totals).astype(jnp.bfloat16)
    attended = jnp.dot(softmax_rows, value_rows, preferred_element_type=jnp.float32)
    return (attended, (highest + jnp.log(totals))[:, 0])


def attend_back(pieces):
    query_rows, key_rows, value_rows, grad_rows, log_totals, deltas, query_segs, key_segs = pieces
    scores = masked_scores(query_rows, key_rows, query_segs, key_segs)
    softmax_rows = jnp.exp(scores - log_totals[:, None])
    grad_softmax = lax.dot_general(
        grad_rows, value_rows, (((1,), (1,)), ((), ())), preferred_element_type=jnp.float32
    )
    grad_scores = (softmax_rows * (grad_softmax - deltas[:, None])).astype(jnp.bfloat16)
    score_scale = HEAD_DIM ** (-0.5)
    grad_query = jnp.dot(grad_scores, key_rows, preferred_element_type=jnp.float32) * score_scale
    grad_keys = (
        lax.dot_general(
            grad_scores, query_rows, (((0,), (0,)), ((), ())), preferred_element_type=jnp.float32
        )
        * score_scale
    )
    grad_values = lax.dot_general(
        softmax_rows.astype(jnp.bfloat16),
        grad_rows,
        (((0,), (0,)), ((), ())),
        preferred_element_type=jnp.float32,
    )
    return (grad_query, grad_keys, grad_values)


def norm_forward(resid, gain, shift):
    row_mean = jnp.mean(resid, axis=2, keepdims=True)
    spread = jnp.mean(resid * resid, axis=2, keepdims=True) - row_mean * row_mean
    inverse = lax.rsqrt(spread + epsilon)
    normed = (resid - row_mean) * inverse
    return (normed * gain + shift, normed, inverse)


def norm_backward(upstream, normed, inverse, gain):
    scaled = upstream * gain
    first_mean = jnp.mean(scaled, axis=2, keepdims=True)
    second_mean = jnp.mean(scaled * normed, axis=2, keepdims=True)
    back_term = inverse * (scaled - first_mean - normed * second_mean)
    return (back_term, jnp.sum(upstream * normed, axis=(0, 1)), jnp.sum(upstream, axis=(0, 1)))


def token_sum(tensor):
    return jnp.sum(tensor.astype(jnp.float32), axis=(0, 1))


def per_device(
    inputs,
    segments,
    query_weight,
    query_bias,
    key_weight,
    value_weight,
    value_bias,
    output_weight,
    output_bias,
    first_gain,
    first_shift,
    expand_weight,
    expand_bias,
    contract_weight,
    contract_bias,
    second_gain,
    second_shift,
    cotangent,
):
    seq_count, rows_here, _ = inputs.shape
    ctx_rows = rows_here * lax.axis_size("tp")
    heads_here = query_weight.shape[1] // HEAD_DIM
    own_segments = lax.dynamic_slice_in_dim(segments, lax.axis_index("ctx") * ctx_rows, ctx_rows, 1)
    query_segs = jnp.repeat(own_segments, heads_here, axis=0)
    key_segs = jnp.repeat(segments, heads_here, axis=0)
    front_set, back_set = fetch_weights(
        query_weight, key_weight, value_weight, expand_weight, output_weight, contract_weight
    )
    query_full, key_full, value_full, expand_full = front_set
    output_full, contract_full = back_set
    inputs_whole = whole_rows(inputs)
    query_low = (
        jnp.einsum("scd,de->sce", inputs_whole, query_full, preferred_element_type=jnp.float32)
        + query_bias
    ).astype(jnp.bfloat16)
    keys_low = jnp.einsum(
        "scd,de->sce", inputs_whole, key_full, preferred_element_type=jnp.float32
    ).astype(jnp.bfloat16)
    values_low = (
        jnp.einsum("scd,de->sce", inputs_whole, value_full, preferred_element_type=jnp.float32)
        + value_bias
    ).astype(jnp.bfloat16)
    keys_all, values_all = fetch_blocks(keys_low, values_low)
    query_items = to_items(query_low)
    attended_items, log_totals = lax.map(
        attend, (query_items, to_items(keys_all), to_items(values_all), query_segs, key_segs)
    )
    attended = from_items(attended_items, seq_count)
    attended_low = attended.astype(jnp.bfloat16)
    branch = (
        feature_sum(
            jnp.einsum("sce,ed->scd", attended_low, output_full, preferred_element_type=jnp.float32)
        )
        + output_bias
    )
    middle, middle_normed, middle_inverse = norm_forward(
        inputs.astype(jnp.float32) + branch, first_gain, first_shift
    )
    middle_whole = whole_rows(middle.astype(jnp.bfloat16))
    preact = (
        jnp.einsum("scd,df->scf", middle_whole, expand_full, preferred_element_type=jnp.float32)
        + expand_bias
    )
    active, gelu_pull = jax.vjp(exact_gelu, preact)
    active_low = active.astype(jnp.bfloat16)
    feedforward = (
        feature_sum(
            jnp.einsum("scf,fd->scd", active_low, contract_full, preferred_element_type=jnp.float32)
        )
        + contract_bias
    )
    outputs, final_normed, final_inverse = norm_forward(
        middle + feedforward, second_gain, second_shift
    )
    front_use, back_use = fetch_weights(
        query_weight, key_weight, value_weight, expand_weight, output_weight, contract_weight
    )
    keys_use, values_use = fetch_blocks(keys_low, values_low)
    query_use, key_use, value_use, expand_use = front_use
    output_use, contract_use = back_use
    final_grad, second_gain_grad, second_shift_grad = norm_backward(
        cotangent.astype(jnp.float32), final_normed, final_inverse, second_gain
    )
    feed_grad = final_grad.astype(jnp.bfloat16)
    contract_bias_grad = token_sum(feed_grad)
    feed_whole = whole_rows(feed_grad)
    contract_part = jnp.einsum(
        "scf,scd->fd", active_low, feed_whole, preferred_element_type=jnp.float32
    )
    active_grad = jnp.einsum(
        "scd,fd->scf", feed_whole, contract_use, preferred_element_type=jnp.float32
    )
    preact_grad = gelu_pull(active_grad)[0].astype(jnp.bfloat16)
    expand_bias_grad = token_sum(preact_grad)
    expand_part = jnp.einsum(
        "scd,scf->df", middle_whole, preact_grad, preferred_element_type=jnp.float32
    )
    middle_grad = final_grad + feature_sum(
        jnp.einsum("scf,df->scd", preact_grad, expand_use, preferred_element_type=jnp.float32)
    )
    resid_grad, first_gain_grad, first_shift_grad = norm_backward(
        middle_grad, middle_normed, middle_inverse, first_gain
    )
    branch_grad = resid_grad.astype(jnp.bfloat16)
    output_bias_grad = token_sum(branch_grad)
    branch_whole = whole_rows(branch_grad)
    output_part = jnp.einsum(
        "sce,scd->ed", attended_low, branch_whole, preferred_element_type=jnp.float32
    )
    attended_grad = jnp.einsum(
        "scd,ed->sce", branch_whole, output_use, preferred_element_type=jnp.float32
    ).astype(jnp.bfloat16)
    deltas = jnp.sum(
        (attended_grad.astype(jnp.float32) * attended).reshape(
            seq_count, ctx_rows, heads_here, HEAD_DIM
        ),
        axis=3,
    ).transpose(0, 2, 1)
    delta_items = deltas.reshape(seq_count * heads_here, ctx_rows)
    grad_items = to_items(attended_grad)
    query_back, keys_part, values_part = lax.map(
        attend_back,
        (
            query_items,
            to_items(keys_use),
            to_items(values_use),
            grad_items,
            log_totals,
            delta_items,
            query_segs,
            key_segs,
        ),
    )
    keys_grad, values_grad = (
        lax.psum_scatter(
            from_items(keys_part, seq_count).astype(jnp.bfloat16),
            "ctx",
            scatter_dimension=1,
            tiled=True,
        ).astype(jnp.float32),
        lax.psum_scatter(
            from_items(values_part, seq_count).astype(jnp.bfloat16),
            "ctx",
            scatter_dimension=1,
            tiled=True,
        ).astype(jnp.float32),
    )
    query_grad = from_items(query_back, seq_count).astype(jnp.bfloat16)
    keys_grad_low = keys_grad.astype(jnp.bfloat16)
    values_grad_low = values_grad.astype(jnp.bfloat16)
    query_bias_grad = token_sum(query_grad)
    value_bias_grad = token_sum(values_grad_low)
    query_part = jnp.einsum(
        "scd,sce->de", inputs_whole, query_grad, preferred_element_type=jnp.float32
    )
    key_part = jnp.einsum(
        "scd,sce->de", inputs_whole, keys_grad_low, preferred_element_type=jnp.float32
    )
    value_part = jnp.einsum(
        "scd,sce->de", inputs_whole, values_grad_low, preferred_element_type=jnp.float32
    )
    input_terms = (
        jnp.einsum("sce,de->scd", query_grad, query_use, preferred_element_type=jnp.float32)
        + jnp.einsum("sce,de->scd", keys_grad_low, key_use, preferred_element_type=jnp.float32)
        + jnp.einsum("sce,de->scd", values_grad_low, value_use, preferred_element_type=jnp.float32)
    )
    input_grad = (resid_grad + feature_sum(input_terms)).astype(jnp.bfloat16)
    query_weight_grad, key_weight_grad, value_weight_grad, expand_weight_grad = in_one_piece(
        (
            query_part.astype(jnp.bfloat16),
            key_part.astype(jnp.bfloat16),
            value_part.astype(jnp.bfloat16),
            expand_part.astype(jnp.bfloat16),
        ),
        ("fsdp", "ctx"),
        0,
        1,
    )
    output_weight_grad, contract_weight_grad = in_one_piece(
        (output_part.astype(jnp.bfloat16), contract_part.astype(jnp.bfloat16)),
        ("fsdp", "ctx"),
        1,
        0,
    )
    column_sums = lax.psum((query_bias_grad, value_bias_grad, expand_bias_grad), ("fsdp", "ctx"))
    whole_sums = lax.psum(
        (
            output_bias_grad,
            first_gain_grad,
            first_shift_grad,
            contract_bias_grad,
            second_gain_grad,
            second_shift_grad,
        ),
        ("fsdp", "ctx", "tp"),
    )
    return (
        outputs.astype(jnp.bfloat16),
        input_grad,
        query_weight_grad,
        column_sums[0],
        key_weight_grad,
        value_weight_grad,
        column_sums[1],
        output_weight_grad,
        whole_sums[0],
        whole_sums[1],
        whole_sums[2],
        expand_weight_grad,
        column_sums[2],
        contract_weight_grad,
        whole_sums[3],
        whole_sums[4],
        whole_sums[5],
    )


def solution(mesh):
    placed = (
        P("fsdp", ("ctx", "tp"), None),
        P("fsdp", None),
        P(("fsdp", "ctx"), "tp"),
        P("tp"),
        P(("fsdp", "ctx"), "tp"),
        P(("fsdp", "ctx"), "tp"),
        P("tp"),
        P("tp", ("fsdp", "ctx")),
        P(),
        P(),
        P(),
        P(("fsdp", "ctx"), "tp"),
        P("tp"),
        P("tp", ("fsdp", "ctx")),
        P(),
        P(),
        P(),
        P("fsdp", ("ctx", "tp"), None),
    )
    return jax.shard_map(
        per_device,
        mesh=mesh,
        in_specs=placed,
        out_specs=(
            P("fsdp", ("ctx", "tp"), None),
            P("fsdp", ("ctx", "tp"), None),
            P(("fsdp", "ctx"), "tp"),
            P("tp"),
            P(("fsdp", "ctx"), "tp"),
            P(("fsdp", "ctx"), "tp"),
            P("tp"),
            P("tp", ("fsdp", "ctx")),
            P(),
            P(),
            P(),
            P(("fsdp", "ctx"), "tp"),
            P("tp"),
            P("tp", ("fsdp", "ctx")),
            P(),
            P(),
            P(),
        ),
        check_vma=False,
    )
```

profile of v0, /device:TPU:0, one launch (start us, length us, event | category | flops | bytes accessed | tf_op | source)
XLA Modules:
  0.0 1107.1 jit_solution(9086204547020164236)
XLA Ops:
  8.8 11.3 %all_gather.48 = bf16[768,192]{1,0:T(8,128)(2,1)S(1)} all-gather(bf16[96,192]{1,0:T(8,128)(2,1)} %param.27), channel_id=1, replica_groups=mesh['fsdp'=2,'ctx'=4,'tp'=4] {'fsdp','ctx'}, dimensions={0}, use_global_device_ids=true | all-gather | bytes 331776 | tf_op jit(solution)/shard_map/all_gather | solution.py:52
  20.1 56.5 %all-gather.9.cloned.1.call-done = bf16[4,512,768]{2,1,0:T(8,128)(2,1)} async-done(((bf16[4,128,768]{2,1,0:T(8,128)(2,1)}), bf16[4,512,768]{2,1,0:T(8,128)(2,1)}) %all-gather.9.cloned.1.call-update) | async-done | bytes 3145744 | tf_op jit(solution)/shard_map/all_gather | solution.py:37
  80.8 9.9 all_gather.46
  100.1 10.6 all_gather.45
  110.7 10.4 all_gather.50
  126.6 4.5 copy.103
  131.2 9.1 all-gather.11.cloned.1.call-done
  142.9 4.5 copy.102
  147.4 137.5 %while.28 = (s32[]{:T(128)}, f32[12,512,64]{1,2,0:T(8,128)}, f32[12,512]{1,0:T(8,128)}, s32[12,512]{1,0:T(8,128)}, s32[12,2048]{1,0:T(8,128)}, /*index=5*/bf16[1...) while((s32[]{:T(128)}, f32[12,512,64]{1,2,0:T(8,128)}, ...), condition=%wide.region_3.4_spmd.clone, body=%wide.region_0.3_spmd.sunk.clone | while | flops 277872128 | bytes 30724220 | solution.py:191
  290.1 59.7 %reduce-scatter.7.cloned.1.call-done = bf16[4,128,768]{2,1,0:T(8,128)(2,1)} async-done(((bf16[4,512,768]{2,1,0:T(8,128)(2,1)}), bf16[4,128,768]{2,1,0:T(8,128)(2,1)}) %reduce-scatter.7.cloned.1.call-update) | async-done | bytes 786448 | tf_op jit(solution)/shard_map/reduce_scatter | solution.py:41
  354.6 62.7 %all-gather.15.cloned.1.call-done = bf16[4,512,768]{2,1,0:T(8,128)(2,1)} async-done(((bf16[4,128,768]{2,1,0:T(8,128)(2,1)}), bf16[4,512,768]{2,1,0:T(8,128)(2,1)}) %all-gather.15.cloned.1.call-update) | async-done | bytes 3145744 | tf_op jit(solution)/shard_map/all_gather | solution.py:37
  417.2 6.4 fusion.51
  426.3 15.6 %multiply_convert_fusion.1 = (bf16[4,512,768]{2,1,0:T(8,128)(2,1)}, f32[4,512,768]{2,1,0:T(8,128)}) fusion(f32[4,512,768]{2,1,0:T(8,128)S(1)} %get-tuple-element.315, f32[768]{0:T(1024)S(1)} %copy-done.37, u8[512,768]{1,0:T(8,128)(4,1)S(1)} %get-tuple-element.221, u8[512,768]{1,0:T(8,128)(4,1)S(1)} %get-tuple-element.220), kind=kLoop, calls=%fused_computation.62 | loop fusion | flops 111673344 | bytes 16518144 | tf_op jit(solution)/shard_map/convert_element_type | solution.py:211
  441.8 6.6 convolution_convert_fusion.2
  448.5 60.1 %reduce-scatter.9.cloned.1.call-done = bf16[4,128,768]{2,1,0:T(8,128)(2,1)} async-done(((bf16[4,512,768]{2,1,0:T(8,128)(2,1)}), bf16[4,128,768]{2,1,0:T(8,128)(2,1)}) %reduce-scatter.9.cloned.1.call-update) | async-done | bytes 786448 | tf_op jit(solution)/shard_map/reduce_scatter | solution.py:41
  516.6 63.0 %all-gather.21.cloned.1.call-done = bf16[4,512,768]{2,1,0:T(8,128)(2,1)} async-done(((bf16[4,128,768]{2,1,0:T(8,128)(2,1)}), bf16[4,512,768]{2,1,0:T(8,128)(2,1)}) %all-gather.21.cloned.1.call-update) | async-done | bytes 3145744 | tf_op jit(solution)/shard_map/all_gather | solution.py:37
  579.6 11.1 convert_reduce_fusion
  596.4 59.1 %reduce-scatter.11.cloned.1.call-done = bf16[4,128,768]{2,1,0:T(8,128)(2,1)} async-done(((bf16[4,512,768]{2,1,0:T(8,128)(2,1)}), bf16[4,128,768]{2,1,0:T(8,128)(2,1)}) %reduce-scatter.11.cloned.1.call-update) | async-done | bytes 786448 | tf_op jit(solution)/shard_map/reduce_scatter | solution.py:41
  655.5 4.2 multiply_reduce_fusion
  663.2 63.3 %all-gather.23.cloned.1.call-done = bf16[4,512,768]{2,1,0:T(8,128)(2,1)} async-done(((bf16[4,128,768]{2,1,0:T(8,128)(2,1)}), bf16[4,512,768]{2,1,0:T(8,128)(2,1)}) %all-gather.23.cloned.1.call-update) | async-done | bytes 3145744 | tf_op jit(solution)/shard_map/all_gather | solution.py:37
  737.0 149.8 %while.29 = (s32[]{:T(128)}, bf16[12,512,64]{1,2,0:T(8,128)(2,1)S(1)}, bf16[12,2048,64]{1,2,0:T(8,128)(2,1)}, bf16[12,2048,64]{1,2,0:T(8,128)(2,1)}, s32[12,512]...) while((s32[]{:T(128)}, ...), condition=%wide.region_17.18_spmd.clone, body=%wide.region_16.17_spmd.sunk.clone | while | flops 679641088 | bytes 22199424 | solution.py:267
  891.8 31.6 %reduce-scatter.13.cloned.1.call-done = bf16[4,512,192]{1,2,0:T(8,128)(2,1)} async-done(((bf16[4,2048,192]{1,2,0:T(8,128)(2,1)}), bf16[4,512,192]{1,2,0:T(8,128)(2,1)}) %reduce-scatter.13.cloned.1.call-update) | async-done | bytes 786448 | tf_op jit(solution)/shard_map/reduce_scatter | solution.py:281
  923.4 4.8 fusion.71
  928.3 35.4 %reduce-scatter.15.cloned.1.call-done = bf16[4,512,192]{1,2,0:T(8,128)(2,1)} async-done(((bf16[4,2048,192]{1,2,0:T(8,128)(2,1)}), bf16[4,512,192]{1,2,0:T(8,128)(2,1)}) %reduce-scatter.15.cloned.1.call-update) | async-done | bytes 786448 | tf_op jit(solution)/shard_map/reduce_scatter | solution.py:287
  963.7 7.6 add_convert_fusion
  971.3 5.7 bitcast_convert_fusion
  984.4 4.3 all-to-all-start.1
  995.2 4.1 copy.84
  999.4 9.4 all-to-all-done.1
  1008.8 4.4 all-to-all-start
  1013.2 60.9 %all-reduce = (f32[768]{0:T(1024)}, f32[768]{0:T(1024)}, f32[768]{0:T(1024)}, f32[768]{0:T(1024)}, f32[768]{0:T(1024)}, /*index=5*/f32[768]{0:T(1024)}) all-reduce(f32[768]{0:T(1024)S(1)} %copy-done.35, f32[768]{0:T(1024)S(1)} %copy-done.33, f32[768]{0:T(1024)S(1)} %copy-done.34, ...), channel_id=1, replica_groups=mesh['fsdp'=2,'ctx'=4,'tp'=4] {'fsdp','ctx','tp'}, use_global_device_ids=true, to_apply=%region_29.30 | all-reduce | flops 4608 | bytes 36864 | tf_op jit(solution)/shard_map/psum | solution.py:332
  1079.2 13.9 %all-reduce.1 = (f32[192]{0:T(256)}, f32[192]{0:T(256)}, f32[768]{0:T(1024)}) all-reduce(f32[192]{0:T(256)S(1)} %reduce_sum.211, f32[192]{0:T(256)S(1)} %convert_reduce_fusion.6, f32[768]{0:T(1024)S(1)} %copy-done.38), channel_id=1, replica_groups=mesh['fsdp'=2,'ctx'=4,'tp'=4] {'fsdp','ctx'}, use_global_device_ids=true, to_apply=%region_24.25 | all-reduce | flops 1152 | bytes 9216 | tf_op jit(solution)/shard_map/psum | solution.py:331
  (387 shorter events, 379.3 us)
Async XLA Ops:
  8.0 68.6 %all-gather.9.cloned.1.call-start = ((), (), s32[]{:S(2)}) async-start(), calls=%async_computation.8 | async-start | bytes 3932160 | tf_op jit(solution)/shard_map/all_gather | solution.py:37
  8.8 115.3 %all-gather.13.cloned.1.call-start = ((), (), s32[]{:S(2)}) async-start(), calls=%async_computation.10 | async-start | bytes 3932160 | tf_op jit(solution)/shard_map/all_gather | solution.py:65
  20.1 60.6 %copy-start.17 = (bf16[768,192]{1,0:T(8,128)(2,1)}, bf16[768,192]{1,0:T(8,128)(2,1)S(1)}, u32[]{:S(2)}) copy-start(bf16[768,192]{1,0:T(8,128)(2,1)S(1)} %all_gather.48) | copy-start | bytes 884740
  80.7 59.6 %all-gather.11.cloned.1.call-start = ((), (), s32[]{:S(2)}) async-start(), calls=%async_computation.9 | async-start | bytes 3932160 | tf_op jit(solution)/shard_map/all_gather | solution.py:64
  90.7 30.5 %copy-start.41 = (f32[192]{0:T(256)S(1)}, f32[192]{0:T(256)}, u32[]{:S(2)}) copy-start(f32[192]{0:T(256)} %param.25) | copy-start | bytes 2308
  92.7 257.1 %reduce-scatter.7.cloned.1.call-start = ((), (), s32[]{:S(2)}) async-start(), calls=%async_computation.11 | async-start | bytes 3932160 | tf_op jit(solution)/shard_map/reduce_scatter | solution.py:41
  147.4 139.1 %copy-start.7 = (bf16[192,768]{0,1:T(8,128)(2,1)S(1)}, bf16[192,768]{0,1:T(8,128)(2,1)}, u32[]{:S(2)}) copy-start(bf16[192,768]{0,1:T(8,128)(2,1)} %all_gather.50) | copy-start | bytes 884740
  286.5 63.3 %copy-start.1 = (bf16[4,128,768]{2,1,0:T(8,128)(2,1)S(1)}, bf16[4,128,768]{2,1,0:T(8,128)(2,1)}, u32[]{:S(2)}) copy-start(bf16[4,128,768]{2,1,0:T(8,128)(2,1)} %param.22) | copy-start | bytes 2359300
  286.5 63.3 %copy-start.20 = (f32[768]{0:T(1024)S(1)}, f32[768]{0:T(1024)}, u32[]{:S(2)}) copy-start(f32[768]{0:T(1024)} %param.30) | copy-start | bytes 9220
  289.2 62.2 %copy-start.21 = (f32[768]{0:T(1024)S(1)}, f32[768]{0:T(1024)}, u32[]{:S(2)}) copy-start(f32[768]{0:T(1024)} %param.31) | copy-start | bytes 9220
  289.2 62.2 %copy-start.36 = (f32[768]{0:T(1024)S(1)}, f32[768]{0:T(1024)}, u32[]{:S(2)}) copy-start(f32[768]{0:T(1024)} %param.32) | copy-start | bytes 9220
  289.3 128.0 %copy-start.37 = (f32[768]{0:T(1024)S(1)}, f32[768]{0:T(1024)}, u32[]{:S(2)}) copy-start(f32[768]{0:T(1024)} %param.34) | copy-start | bytes 9220
  289.3 65.3 %all-gather.17.cloned.1.call-start = ((), (), s32[]{:S(2)}) async-start(), calls=%async_computation.13 | async-start | bytes 1327104 | tf_op jit(solution)/shard_map/all_gather | solution.py:53
  289.8 127.4 %all-gather.15.cloned.1.call-start = ((), (), s32[]{:S(2)}) async-start(), calls=%async_computation.12 | async-start | bytes 3932160 | tf_op jit(solution)/shard_map/all_gather | solution.py:37
  353.9 87.9 %all-gather.19.cloned.1.call-start = ((), (), s32[]{:S(2)}) async-start(), calls=%async_computation.14 | async-start | bytes 1327104 | tf_op jit(solution)/shard_map/all_gather | solution.py:57
  354.5 154.1 %reduce-scatter.9.cloned.1.call-start = ((), (), s32[]{:S(2)}) async-start(), calls=%async_computation.15 | async-start | bytes 3932160 | tf_op jit(solution)/shard_map/reduce_scatter | solution.py:41
  448.4 60.2 %copy-start.2 = (bf16[4,128,768]{2,1,0:T(8,128)(2,1)S(1)}, bf16[4,128,768]{2,1,0:T(8,128)(2,1)}, u32[]{:S(2)}) copy-start(bf16[4,128,768]{2,1,0:T(8,128)(2,1)} %reduce-scatter.7.cloned.1.call-done) | copy-start | bytes 2359300
  448.5 131.1 %all-gather.21.cloned.1.call-start = ((), (), s32[]{:S(2)}) async-start(), calls=%async_computation.16 | async-start | bytes 3932160 | tf_op jit(solution)/shard_map/all_gather | solution.py:37
  516.3 139.2 %reduce-scatter.11.cloned.1.call-start = ((), (), s32[]{:S(2)}) async-start(), calls=%async_computation.17 | async-start | bytes 3932160 | tf_op jit(solution)/shard_map/reduce_scatter | solution.py:41
  596.4 130.1 %all-gather.23.cloned.1.call-start = ((), (), s32[]{:S(2)}) async-start(), calls=%async_computation.18 | async-start | bytes 3932160 | tf_op jit(solution)/shard_map/all_gather | solution.py:37
  659.7 66.8 %copy-start.8 = (bf16[192,768]{0,1:T(8,128)(2,1)S(1)}, bf16[192,768]{0,1:T(8,128)(2,1)}, u32[]{:S(2)}) copy-start(bf16[192,768]{0,1:T(8,128)(2,1)} %all_gather.50) | copy-start | bytes 884740
  659.7 70.0 %copy-start.24 = (f32[4,128]{1,0:T(4,128)}, f32[4,128]{1,0:T(4,128)S(1)}, u32[]{:S(2)}) copy-start(f32[4,128]{1,0:T(4,128)S(1)} %broadcast_multiply_fusion) | copy-start | bytes 6148
  659.7 70.0 %copy-start.26 = (f32[4,128]{1,0:T(4,128)}, f32[4,128]{1,0:T(4,128)S(1)}, u32[]{:S(2)}) copy-start(f32[4,128]{1,0:T(4,128)S(1)} %broadcast_multiply_fusion.1) | copy-start | bytes 6148
  663.0 260.4 %reduce-scatter.13.cloned.1.call-start = ((), (), s32[]{:S(2)}) async-start(), calls=%async_computation.19 | async-start | bytes 3932160 | tf_op jit(solution)/shard_map/reduce_scatter | solution.py:281
  886.9 76.8 %reduce-scatter.15.cloned.1.call-start = ((), (), s32[]{:S(2)}) async-start(), calls=%async_computation.20 | async-start | bytes 3932160 | tf_op jit(solution)/shard_map/reduce_scatter | solution.py:287
  887.7 209.0 %reduce-scatter.17.cloned.1.call-start = ((), (), s32[]{:S(2)}) async-start(), calls=%async_computation.21 | async-start | bytes 3932160 | tf_op jit(solution)/shard_map/reduce_scatter | solution.py:41
  891.8 71.9 %copy-start.18 = (bf16[768,192]{1,0:T(8,128)(2,1)S(1)}, bf16[768,192]{1,0:T(8,128)(2,1)}, u32[]{:S(2)}) copy-start(bf16[768,192]{1,0:T(8,128)(2,1)} %copy-done.17) | copy-start | bytes 884740
  984.4 24.4 %all-to-all-start.1 = ((bf16[8,960,96]{1,2,0:T(8,128)(2,1)}), bf16[8,960,96]{1,2,0:T(8,128)(2,1)}, u32[]{:S(2)}, u32[]{:S(2)}) async-start(bf16[8,960,96]{1,2,0:T(8,128)(2,1)} %bitcast.258), calls=%async_computation.7 | async-start | bytes 3145728 | tf_op jit(solution)/shard_map/all_to_all | solution.py:19
  1008.8 84.3 %all-to-all-start = ((bf16[8,96,1344]{2,1,0:T(8,128)(2,1)}), bf16[8,96,1344]{2,1,0:T(8,128)(2,1)}, u32[]{:S(2)}, u32[]{:S(2)}) async-start(bf16[8,96,1344]{2,1,0:T(8,128)(2,1)} %bitcast.255), calls=%async_computation.6 | async-start | bytes 4325376 | tf_op jit(solution)/shard_map/all_to_all | solution.py:19
  1013.2 66.0 %copy-start.38 = (f32[768]{0:T(1024)S(1)}, f32[768]{0:T(1024)}, u32[]{:S(2)}) copy-start(f32[768]{0:T(1024)} %get-tuple-element.316) | copy-start | bytes 9220
  1076.2 20.5 %copy-start.4 = (f32[4,128,768]{2,1,0:T(8,128)S(1)}, f32[4,128,768]{2,1,0:T(8,128)}, u32[]{:S(2)}) copy-start(f32[4,128,768]{2,1,0:T(8,128)} %copy-done.3) | copy-start | bytes 4718596
  1076.2 20.5 %copy-start.25 = (f32[4,128]{1,0:T(4,128)S(1)}, f32[4,128]{1,0:T(4,128)}, u32[]{:S(2)}) copy-start(f32[4,128]{1,0:T(4,128)} %copy-done.24) | copy-start | bytes 6148
  (39 other events, 217.0 us)
Sparse Core Ops, SparseCore 0:
  10.4 66.1 all-gather.8
  80.9 27.7 all-gather.12
  110.8 29.4 all-gather.10
  289.4 60.3 reduce-scatter.6
  663.1 63.2 all-gather.22
  887.0 36.3 reduce-scatter.12
  926.0 37.7 reduce-scatter.14
Sparse Core Ops, SparseCore 1:
  291.6 23.8 all-gather.16
  354.0 63.2 all-gather.14
  419.0 22.4 all-gather.18
  448.5 60.0 reduce-scatter.8
  516.4 63.1 all-gather.20
  596.4 59.0 reduce-scatter.10
  971.4 60.3 reduce-scatter.16
where the time goes:
time: 1120 us; the launch traced here: 1110 us
  waiting for transfers between devices  513 us (46%)
  matrix products  263 us (23%)
  local copies, waits for them, and re-layouts  128 us (11%)
  blocking collectives  117 us (10%)
  other arithmetic  59.3 us (5%)
  between operations  16.5 us (1%)
    all_gather x4, waiting for transfers between devices, whole_rows(): return lax.all_gather(tensor, 'tp', axis=1, tiled=True)  245 us
    reduce_scatter x4, waiting for transfers between devices, feature_sum(): lax.psum_scatter(tensor.astype(jnp.bfloat16), 'tp', scatter_dimension=1,...  179 us
    psum x1, blocking collectives, per_device(): lax.psum((output_bias_grad, first_gain_grad, first_shift_grad, contract_b...  60.9 us
    dot_general x24, matrix products, masked_scores(): lax.dot_general(query_rows, key_rows, (((1,), (1,)), ((), ())), preferred...  49.7 us
    dot_general x12, matrix products, attend(): jnp.dot(softmax_rows, value_rows, preferred_element_type=jnp.float32)  47.1 us
    dynamic_slice x48, local copies, waits for them, and re-layouts, per_device(): lax.map(attend, (query_items, to_items(keys_all), to_items(values_all), q...  37.8 us
    reduce_scatter x1, waiting for transfers between devices, per_device(): lax.psum_scatter(from_items(values_part, seq_count).astype(jnp.bfloat16),...  35.4 us
    reduce_scatter x1, waiting for transfers between devices, per_device(): lax.psum_scatter(from_items(keys_part, seq_count).astype(jnp.bfloat16), '...  31.6 us
  transfers between devices with their start and end apart: 16, of which 11 were waited for; matrix products, arithmetic and copies ran while one was open for 8% of the time, Pallas kernels for 0%

commit v1 on v0

--- a/solution.py
+++ b/solution.py
@@ -6,6 +6,18 @@
 HEAD_DIM = 64
 epsilon = 1e-05
 masked_value = -1e30
+
+
+def gather_by_bits(value, axis, dim):
+    ways, here = (lax.axis_size(axis), lax.axis_index(axis))
+    grown, reach = (value, 1)
+    while reach < ways:
+        theirs = lax.ppermute(grown, axis, [(d, d ^ reach) for d in range(ways)])
+        mine_first = jnp.concatenate([grown, theirs], axis=dim)
+        theirs_first = jnp.concatenate([theirs, grown], axis=dim)
+        grown = jnp.where(here & reach == 0, mine_first, theirs_first)
+        reach = 2 * reach
+    return grown
 
 
 def in_blocks(value, dim, count):
@@ -34,7 +46,7 @@
 
 
 def whole_rows(tensor):
-    return lax.all_gather(tensor, "tp", axis=1, tiled=True)
+    return gather_by_bits(tensor, "tp", 1)
 
 
 def feature_sum(tensor):

time: 1120 us -> 1230 us (1.098)
  waiting for transfers between devices: 513 us -> 594 us
  starting transfers between devices: 10 us -> 26.7 us
    ppermute x0 -> x8, waiting for transfers between devices: none -> 330 us  [gather_by_bits(): theirs = lax.ppermute(grown, axis, [(d, d ^ reach) for d in range(ways)])]
    all_gather x4 -> x0, waiting for transfers between devices: 245 us -> none  [whole_rows(): return lax.all_gather(tensor, 'tp', axis=1, tiled=True)]
    ppermute x0 -> x8, starting transfers between devices: none -> 16.8 us  [gather_by_bits(): theirs = lax.ppermute(grown, axis, [(d, d ^ reach) for d in range(ways)])]
  transfers between devices with their start and end apart: 16 -> 20, of which waited for: 11 -> 16; matrix products, arithmetic and copies ran while one was open for 8% -> 8% of each run, Pallas kernels for 0% -> 0%
where the time goes in v1:
time: 1230 us; the launch traced here: 1220 us
  waiting for transfers between devices  594 us (48%)
  matrix products  267 us (22%)
  local copies, waits for them, and re-layouts  129 us (10%)
  blocking collectives  116 us (9%)
  other arithmetic  66.6 us (5%)
  starting transfers between devices  26.7 us (2%)
  between operations  16.8 us (1%)
    ppermute x8, waiting for transfers between devices, gather_by_bits(): theirs = lax.ppermute(grown, axis, [(d, d ^ reach) for d in range(ways)])  330 us
    reduce_scatter x4, waiting for transfers between devices, feature_sum(): lax.psum_scatter(tensor.astype(jnp.bfloat16), 'tp', scatter_dimension=1,...  181 us
    psum x1, blocking collectives, per_device(): lax.psum((output_bias_grad, first_gain_grad, first_shift_grad, contract_b...  60.9 us
    dot_general x24, matrix products, masked_scores(): lax.dot_general(query_rows, key_rows, (((1,), (1,)), ((), ())), preferred...  48.8 us
    dot_general x12, matrix products, attend(): jnp.dot(softmax_rows, value_rows, preferred_element_type=jnp.float32)  39.2 us
    dynamic_slice x48, local copies, waits for them, and re-layouts, per_device(): lax.map(attend, (query_items, to_items(keys_all), to_items(values_all), q...  37.8 us
    reduce_scatter x1, waiting for transfers between devices, per_device(): lax.psum_scatter(from_items(values_part, seq_count).astype(jnp.bfloat16),...  35.5 us
    reduce_scatter x1, waiting for transfers between devices, per_device(): lax.psum_scatter(from_items(keys_part, seq_count).astype(jnp.bfloat16), '...  33.2 us
  transfers between devices with their start and end apart: 20, of which 16 were waited for; matrix products, arithmetic and copies ran while one was open for 8% of the time, Pallas kernels for 0%

profile of v1, /device:TPU:0, one launch (start us, length us, event | category | flops | bytes accessed | tf_op | source)
XLA Modules:
  0.0 1216.7 jit_solution(10606072545417409633)
XLA Ops:
  11.2 17.8 %collective-permute-done = bf16[4,128,768]{2,1,0:T(8,128)(2,1)S(1)} collective-permute-done((bf16[4,128,768]{2,1,0:T(8,128)(2,1)}, bf16[4,128,768]{2,1,0:T(8,128)(2,1)S(1)}, u32[]{:S(2)}, u32[]{:S(2)}) %collective-permute-start) | collective-permute-done | bytes 786464 | tf_op jit(solution)/shard_map/ppermute | solution.py:15
  33.7 9.6 all_gather.35
  43.2 57.9 %collective-permute-done.1 = bf16[4,256,768]{2,1,0:T(8,128)(2,1)} collective-permute-done((bf16[4,256,768]{2,1,0:T(8,128)(2,1)S(1)}, bf16[4,256,768]{2,1,0:T(8,128)(2,1)}, u32[]{:S(2)}, u32[]{:S(2)}) %collective-permute-start.1) | collective-permute-done | bytes 1572896 | tf_op jit(solution)/shard_map/ppermute | solution.py:15
  105.2 9.5 all_gather.33
  121.1 11.5 all_gather.32
  132.6 11.0 all_gather.37
  153.8 6.6 copy.103
  160.4 6.7 all-gather.5.cloned.1.call-done
  171.2 6.6 copy.102
  177.8 129.3 %while.28 = (s32[]{:T(128)}, f32[12,512,64]{1,2,0:T(8,128)S(1)}, f32[12,512]{1,0:T(8,128)}, s32[12,512]{1,0:T(8,128)}, s32[12,2048]{1,0:T(8,128)}, /*index=5*/bf...) while((s32[]{:T(128)}, f32[12,512,64]{1,2,0:T(8,128)S(1)}, ...), condition=%wide.region_3.4_spmd.clone, body=%wide.region_0.3_spmd.sunk.clone | while | flops 277872128 | bytes 30724220 | solution.py:203
  313.1 60.5 %reduce-scatter.7.cloned.1.call-done = bf16[4,128,768]{2,1,0:T(8,128)(2,1)} async-done(((bf16[4,512,768]{2,1,0:T(8,128)(2,1)}), bf16[4,128,768]{2,1,0:T(8,128)(2,1)}) %reduce-scatter.7.cloned.1.call-update) | async-done | bytes 786448 | tf_op jit(solution)/shard_map/reduce_scatter | solution.py:53
  377.8 18.1 %collective-permute-done.2 = bf16[4,128,768]{2,1,0:T(8,128)(2,1)} collective-permute-done((bf16[4,128,768]{2,1,0:T(8,128)(2,1)S(1)}, bf16[4,128,768]{2,1,0:T(8,128)(2,1)}, u32[]{:S(2)}, u32[]{:S(2)}) %collective-permute-start.2) | collective-permute-done | bytes 786464 | tf_op jit(solution)/shard_map/ppermute | solution.py:15
  402.2 65.8 %collective-permute-done.3 = bf16[4,256,768]{2,1,0:T(8,128)(2,1)} collective-permute-done((bf16[4,256,768]{2,1,0:T(8,128)(2,1)S(1)}, bf16[4,256,768]{2,1,0:T(8,128)(2,1)}, u32[]{:S(2)}, u32[]{:S(2)}) %collective-permute-start.3) | collective-permute-done | bytes 1572896 | tf_op jit(solution)/shard_map/ppermute | solution.py:15
  468.0 6.5 fusion.51
  477.1 16.3 %multiply_convert_fusion.1 = (bf16[4,512,768]{2,1,0:T(8,128)(2,1)}, f32[4,512,768]{2,1,0:T(8,128)}) fusion(f32[4,512,768]{2,1,0:T(8,128)S(1)} %get-tuple-element.315, f32[768]{0:T(1024)} %param.34, u8[512,768]{1,0:T(8,128)(4,1)S(1)} %get-tuple-element.221, u8[512,768]{1,0:T(8,128)(4,1)S(1)} %get-tuple-element.220), kind=kLoop, calls=%fused_computation.62 | loop fusion | flops 111673344 | bytes 16518144 | tf_op jit(solution)/shard_map/convert_element_type | solution.py:223
  493.4 6.6 convolution_convert_fusion.2
  500.1 60.4 %reduce-scatter.9.cloned.1.call-done = bf16[4,128,768]{2,1,0:T(8,128)(2,1)} async-done(((bf16[4,512,768]{2,1,0:T(8,128)(2,1)}), bf16[4,128,768]{2,1,0:T(8,128)(2,1)}) %reduce-scatter.9.cloned.1.call-update) | async-done | bytes 786448 | tf_op jit(solution)/shard_map/reduce_scatter | solution.py:53
  568.7 18.0 %collective-permute-done.4 = bf16[4,128,768]{2,1,0:T(8,128)(2,1)S(1)} collective-permute-done((bf16[4,128,768]{2,1,0:T(8,128)(2,1)S(1)}, bf16[4,128,768]{2,1,0:T(8,128)(2,1)S(1)}, u32[]{:S(2)}, u32[]{:S(2)}) %collective-permute-start.4) | collective-permute-done | bytes 786464 | tf_op jit(solution)/shard_map/ppermute | solution.py:15
  590.1 67.2 %collective-permute-done.5 = bf16[4,256,768]{2,1,0:T(8,128)(2,1)S(1)} collective-permute-done((bf16[4,256,768]{2,1,0:T(8,128)(2,1)S(1)}, bf16[4,256,768]{2,1,0:T(8,128)(2,1)S(1)}, u32[]{:S(2)}, u32[]{:S(2)}) %collective-permute-start.5) | collective-permute-done | bytes 1572896 | tf_op jit(solution)/shard_map/ppermute | solution.py:15
  657.3 7.4 convert_reduce_fusion
  670.7 60.3 %reduce-scatter.11.cloned.1.call-done = bf16[4,128,768]{2,1,0:T(8,128)(2,1)} async-done(((bf16[4,512,768]{2,1,0:T(8,128)(2,1)}), bf16[4,128,768]{2,1,0:T(8,128)(2,1)}) %reduce-scatter.11.cloned.1.call-update) | async-done | bytes 786448 | tf_op jit(solution)/shard_map/reduce_scatter | solution.py:53
  738.6 18.0 %collective-permute-done.6 = bf16[4,128,768]{2,1,0:T(8,128)(2,1)S(1)} collective-permute-done((bf16[4,128,768]{2,1,0:T(8,128)(2,1)S(1)}, bf16[4,128,768]{2,1,0:T(8,128)(2,1)S(1)}, u32[]{:S(2)}, u32[]{:S(2)}) %collective-permute-start.6) | collective-permute-done | bytes 786464 | tf_op jit(solution)/shard_map/ppermute | solution.py:15
  761.2 67.4 %collective-permute-done.7 = bf16[4,256,768]{2,1,0:T(8,128)(2,1)} collective-permute-done((bf16[4,256,768]{2,1,0:T(8,128)(2,1)}, bf16[4,256,768]{2,1,0:T(8,128)(2,1)}, u32[]{:S(2)}, u32[]{:S(2)}) %collective-permute-start.7) | collective-permute-done | bytes 1572896 | tf_op jit(solution)/shard_map/ppermute | solution.py:15
  840.2 149.7 %while.29 = (s32[]{:T(128)}, bf16[12,512,64]{1,2,0:T(8,128)(2,1)S(1)}, bf16[12,2048,64]{1,2,0:T(8,128)(2,1)}, bf16[12,2048,64]{1,2,0:T(8,128)(2,1)}, s32[12,512]...) while((s32[]{:T(128)}, ...), condition=%wide.region_17.18_spmd.clone, body=%wide.region_16.17_spmd.sunk.clone | while | flops 679641088 | bytes 22199424 | solution.py:279
  994.7 33.2 %reduce-scatter.13.cloned.1.call-done = bf16[4,512,192]{1,2,0:T(8,128)(2,1)} async-done(((bf16[4,2048,192]{1,2,0:T(8,128)(2,1)}), bf16[4,512,192]{1,2,0:T(8,128)(2,1)}) %reduce-scatter.13.cloned.1.call-update) | async-done | bytes 786448 | tf_op jit(solution)/shard_map/reduce_scatter | solution.py:293
  1028.0 4.8 fusion.68
  1032.8 35.5 %reduce-scatter.15.cloned.1.call-done = bf16[4,512,192]{1,2,0:T(8,128)(2,1)} async-done(((bf16[4,2048,192]{1,2,0:T(8,128)(2,1)}), bf16[4,512,192]{1,2,0:T(8,128)(2,1)}) %reduce-scatter.15.cloned.1.call-update) | async-done | bytes 786448 | tf_op jit(solution)/shard_map/reduce_scatter | solution.py:299
  1068.3 7.5 add_convert_fusion
  1075.9 6.8 bitcast_convert_fusion.1
  1093.4 4.6 all-to-all-start.1
  1122.5 60.9 %all-reduce = (f32[768]{0:T(1024)}, f32[768]{0:T(1024)}, f32[768]{0:T(1024)}, f32[768]{0:T(1024)}, f32[768]{0:T(1024)}, /*index=5*/f32[768]{0:T(1024)}) all-reduce(f32[768]{0:T(1024)S(1)} %copy-done.44, f32[768]{0:T(1024)S(1)} %copy-done.42, f32[768]{0:T(1024)S(1)} %copy-done.43, ...), channel_id=1, replica_groups=mesh['fsdp'=2,'ctx'=4,'tp'=4] {'fsdp','ctx','tp'}, use_global_device_ids=true, to_apply=%region_29.30 | all-reduce | flops 4608 | bytes 36864 | tf_op jit(solution)/shard_map/psum | solution.py:344
  1188.4 13.9 %all-reduce.1 = (f32[192]{0:T(256)}, f32[192]{0:T(256)}, f32[768]{0:T(1024)}) all-reduce(f32[192]{0:T(256)S(1)} %reduce_sum.211, f32[192]{0:T(256)S(1)} %convert_reduce_fusion.6, f32[768]{0:T(1024)S(1)} %copy-done.47), channel_id=1, replica_groups=mesh['fsdp'=2,'ctx'=4,'tp'=4] {'fsdp','ctx'}, use_global_device_ids=true, to_apply=%region_24.25 | all-reduce | flops 1152 | bytes 9216 | tf_op jit(solution)/shard_map/psum | solution.py:343
  (420 shorter events, 422.2 us)
Async XLA Ops:
  8.0 93.2 %copy-start.51 = (f32[192]{0:T(256)S(1)}, f32[192]{0:T(256)}, u32[]{:S(2)}) copy-start(f32[192]{0:T(256)} %param.28) | copy-start | bytes 2308
  8.0 141.7 %all-gather.7.cloned.1.call-start = ((), (), s32[]{:S(2)}) async-start(), calls=%async_computation.9 | async-start | bytes 3932160 | tf_op jit(solution)/shard_map/all_gather | solution.py:77
  8.1 20.9 %collective-permute-start = (bf16[4,128,768]{2,1,0:T(8,128)(2,1)}, bf16[4,128,768]{2,1,0:T(8,128)(2,1)S(1)}, u32[]{:S(2)}, u32[]{:S(2)}) collective-permute-start(bf16[4,128,768]{2,1,0:T(8,128)(2,1)} %param.22), channel_id=1, source_target_pairs={{0,1},{1,0},{2,3},{3,2},{4,5},{5,4},{6,7},{7,6},{8,9},{9,8},{10,11... | collective-permute-start | bytes 2359304 | tf_op jit(solution)/shard_map/ppermute | solution.py:15
  30.8 112.8 %copy-start.17 = (bf16[4,256,768]{2,1,0:T(8,128)(2,1)}, bf16[4,256,768]{2,1,0:T(8,128)(2,1)S(1)}, u32[]{:S(2)}) copy-start(bf16[4,256,768]{2,1,0:T(8,128)(2,1)S(1)} %maximum_select_fusion.4) | copy-start | bytes 4718596
  30.8 70.3 %collective-permute-start.1 = (bf16[4,256,768]{2,1,0:T(8,128)(2,1)S(1)}, bf16[4,256,768]{2,1,0:T(8,128)(2,1)}, u32[]{:S(2)}, u32[]{:S(2)}) collective-permute-start(bf16[4,256,768]{2,1,0:T(8,128)(2,1)S(1)} %maximum_select_fusion.4), channel_id=1, source_target_pairs={{0,2},{1,3},{2,0},{3,1},{4,6},{5,7},{6,4},{7,5},{8,10},{9,11},{10,... | collective-permute-start | bytes 4718600 | tf_op jit(solution)/shard_map/ppermute | solution.py:15
  105.2 61.9 %all-gather.5.cloned.1.call-start = ((), (), s32[]{:S(2)}) async-start(), calls=%async_computation.8 | async-start | bytes 3932160 | tf_op jit(solution)/shard_map/all_gather | solution.py:76
  118.9 254.7 %reduce-scatter.7.cloned.1.call-start = ((), (), s32[]{:S(2)}) async-start(), calls=%async_computation.10 | async-start | bytes 3932160 | tf_op jit(solution)/shard_map/reduce_scatter | solution.py:53
  313.0 89.1 %all-gather.9.cloned.1.call-start = ((), (), s32[]{:S(2)}) async-start(), calls=%async_computation.11 | async-start | bytes 1327104 | tf_op jit(solution)/shard_map/all_gather | solution.py:65
  376.8 19.1 %collective-permute-start.2 = (bf16[4,128,768]{2,1,0:T(8,128)(2,1)S(1)}, bf16[4,128,768]{2,1,0:T(8,128)(2,1)}, u32[]{:S(2)}, u32[]{:S(2)}) collective-permute-start(bf16[4,128,768]{2,1,0:T(8,128)(2,1)S(1)} %fusion.52), channel_id=1, source_target_pairs={{0,1},{1,0},{2,3},{3,2},{4,5},{5,4},{6,7},{7,6},{8,9},{9,8},{10,11... | collective-permute-start | bytes 2359304 | tf_op jit(solution)/shard_map/ppermute | solution.py:15
  377.8 115.7 %all-gather.11.cloned.1.call-start = ((), (), s32[]{:S(2)}) async-start(), calls=%async_computation.12 | async-start | bytes 1327104 | tf_op jit(solution)/shard_map/all_gather | solution.py:69
  397.8 76.7 %copy-start.19 = (bf16[4,256,768]{2,1,0:T(8,128)(2,1)}, bf16[4,256,768]{2,1,0:T(8,128)(2,1)S(1)}, u32[]{:S(2)}) copy-start(bf16[4,256,768]{2,1,0:T(8,128)(2,1)S(1)} %maximum_select_fusion.5) | copy-start | bytes 4718596
  397.8 70.2 %collective-permute-start.3 = (bf16[4,256,768]{2,1,0:T(8,128)(2,1)S(1)}, bf16[4,256,768]{2,1,0:T(8,128)(2,1)}, u32[]{:S(2)}, u32[]{:S(2)}) collective-permute-start(bf16[4,256,768]{2,1,0:T(8,128)(2,1)S(1)} %maximum_select_fusion.5), channel_id=1, source_target_pairs={{0,2},{1,3},{2,0},{3,1},{4,6},{5,7},{6,4},{7,5},{8,10},{9,11},{10,... | collective-permute-start | bytes 4718600 | tf_op jit(solution)/shard_map/ppermute | solution.py:15
  400.5 160.0 %reduce-scatter.9.cloned.1.call-start = ((), (), s32[]{:S(2)}) async-start(), calls=%async_computation.13 | async-start | bytes 3932160 | tf_op jit(solution)/shard_map/reduce_scatter | solution.py:53
  500.1 231.0 %reduce-scatter.11.cloned.1.call-start = ((), (), s32[]{:S(2)}) async-start(), calls=%async_computation.14 | async-start | bytes 3932160 | tf_op jit(solution)/shard_map/reduce_scatter | solution.py:53
  560.5 96.7 %slice-start = ((s8[6291456]{0:T(1024)(128)(4,1)}), s8[4194304]{0:T(1024)(128)(4,1)S(1)}, s32[]{:S(2)}) async-start(s8[6291456]{0:T(1024)(128)(4,1)} %bitcast.234), calls=%async_computation.18 | async-start | bytes 8388608
  562.7 94.6 %slice-start.1 = ((s8[6291456]{0:T(1024)(128)(4,1)}), s8[2097152]{0:T(1024)(128)(4,1)S(1)}, s32[]{:S(2)}) async-start(s8[6291456]{0:T(1024)(128)(4,1)} %bitcast.234), calls=%async_computation.19 | async-start | bytes 4194304
  565.3 92.0 %copy-start.6 = (f32[4,512,768]{2,1,0:T(8,128)S(1)}, f32[4,512,768]{2,1,0:T(8,128)}, u32[]{:S(2)}) copy-start(f32[4,512,768]{2,1,0:T(8,128)} %get-tuple-element.290) | copy-start | bytes 18874372
  565.3 92.0 %copy-start.46 = (f32[768]{0:T(1024)S(1)}, f32[768]{0:T(1024)}, u32[]{:S(2)}) copy-start(f32[768]{0:T(1024)} %param.34) | copy-start | bytes 9220
  567.8 18.9 %collective-permute-start.4 = (bf16[4,128,768]{2,1,0:T(8,128)(2,1)S(1)}, bf16[4,128,768]{2,1,0:T(8,128)(2,1)S(1)}, u32[]{:S(2)}, u32[]{:S(2)}) collective-permute-start(bf16[4,128,768]{2,1,0:T(8,128)(2,1)S(1)} %get-tuple-element.284), channel_id=1, source_target_pairs={{0,1},{1,0},{2,3},{3,2},{4,5},{5,4},{6,7},{7,6},{8,9},{9,8},{10,11... | collective-permute-start | bytes 2359304 | tf_op jit(solution)/shard_map/ppermute | solution.py:15
  587.3 77.4 %copy-start.20 = (bf16[4,256,768]{2,1,0:T(8,128)(2,1)}, bf16[4,256,768]{2,1,0:T(8,128)(2,1)S(1)}, u32[]{:S(2)}) copy-start(bf16[4,256,768]{2,1,0:T(8,128)(2,1)S(1)} %maximum_select_fusion.6) | copy-start | bytes 4718596
  587.3 69.9 %collective-permute-start.5 = (bf16[4,256,768]{2,1,0:T(8,128)(2,1)S(1)}, bf16[4,256,768]{2,1,0:T(8,128)(2,1)S(1)}, u32[]{:S(2)}, u32[]{:S(2)}) collective-permute-start(bf16[4,256,768]{2,1,0:T(8,128)(2,1)S(1)} %maximum_select_fusion.6), channel_id=1, source_target_pairs={{0,2},{1,3},{2,0},{3,1},{4,6},{5,7},{6,4},{7,5},{8,10},{9,11},{10,... | collective-permute-start | bytes 4718600 | tf_op jit(solution)/shard_map/ppermute | solution.py:15
  670.4 357.5 %reduce-scatter.13.cloned.1.call-start = ((), (), s32[]{:S(2)}) async-start(), calls=%async_computation.15 | async-start | bytes 3932160 | tf_op jit(solution)/shard_map/reduce_scatter | solution.py:293
  736.4 92.2 %copy-start.16 = (bf16[192,768]{0,1:T(8,128)(2,1)S(1)}, bf16[192,768]{0,1:T(8,128)(2,1)}, u32[]{:S(2)}) copy-start(bf16[192,768]{0,1:T(8,128)(2,1)} %all_gather.37) | copy-start | bytes 884740
  737.7 18.9 %collective-permute-start.6 = (bf16[4,128,768]{2,1,0:T(8,128)(2,1)S(1)}, bf16[4,128,768]{2,1,0:T(8,128)(2,1)S(1)}, u32[]{:S(2)}, u32[]{:S(2)}) collective-permute-start(bf16[4,128,768]{2,1,0:T(8,128)(2,1)S(1)} %get-tuple-element.286), channel_id=1, source_target_pairs={{0,1},{1,0},{2,3},{3,2},{4,5},{5,4},{6,7},{7,6},{8,9},{9,8},{10,11... | collective-permute-start | bytes 2359304 | tf_op jit(solution)/shard_map/ppermute | solution.py:15
  758.4 70.1 %collective-permute-start.7 = (bf16[4,256,768]{2,1,0:T(8,128)(2,1)}, bf16[4,256,768]{2,1,0:T(8,128)(2,1)}, u32[]{:S(2)}, u32[]{:S(2)}) collective-permute-start(bf16[4,256,768]{2,1,0:T(8,128)(2,1)} %maximum_select_fusion.7), channel_id=1, source_target_pairs={{0,2},{1,3},{2,0},{3,1},{4,6},{5,7},{6,4},{7,5},{8,10},{9,11},{10,... | collective-permute-start | bytes 4718600 | tf_op jit(solution)/shard_map/ppermute | solution.py:15
  761.2 72.6 %copy-start.8 = (f32[12,512,64]{1,2,0:T(8,128)S(1)}, f32[12,512,64]{1,2,0:T(8,128)}, u32[]{:S(2)}) copy-start(f32[12,512,64]{1,2,0:T(8,128)} %copy-done.7) | copy-start | bytes 4718596
  989.9 78.3 %reduce-scatter.15.cloned.1.call-start = ((), (), s32[]{:S(2)}) async-start(), calls=%async_computation.16 | async-start | bytes 3932160 | tf_op jit(solution)/shard_map/reduce_scatter | solution.py:299
  990.7 215.2 %reduce-scatter.17.cloned.1.call-start = ((), (), s32[]{:S(2)}) async-start(), calls=%async_computation.17 | async-start | bytes 3932160 | tf_op jit(solution)/shard_map/reduce_scatter | solution.py:53
  994.7 73.5 %copy-start.23 = (bf16[768,192]{1,0:T(8,128)(2,1)S(1)}, bf16[768,192]{1,0:T(8,128)(2,1)}, u32[]{:S(2)}) copy-start(bf16[768,192]{1,0:T(8,128)(2,1)} %copy-done.22) | copy-start | bytes 884740
  1093.4 24.7 %all-to-all-start.1 = ((bf16[8,960,96]{1,2,0:T(8,128)(2,1)}), bf16[8,960,96]{1,2,0:T(8,128)(2,1)}, u32[]{:S(2)}, u32[]{:S(2)}) async-start(bf16[8,960,96]{1,2,0:T(8,128)(2,1)} %bitcast.236), calls=%async_computation.7 | async-start | bytes 3145728 | tf_op jit(solution)/shard_map/all_to_all | solution.py:31
  1118.1 84.3 %all-to-all-start = ((bf16[8,96,1344]{2,1,0:T(8,128)(2,1)}), bf16[8,96,1344]{2,1,0:T(8,128)(2,1)}, u32[]{:S(2)}, u32[]{:S(2)}) async-start(bf16[8,96,1344]{2,1,0:T(8,128)(2,1)} %bitcast.231), calls=%async_computation.6 | async-start | bytes 4325376 | tf_op jit(solution)/shard_map/all_to_all | solution.py:31
  1122.4 66.0 %copy-start.47 = (f32[768]{0:T(1024)S(1)}, f32[768]{0:T(1024)}, u32[]{:S(2)}) copy-start(f32[768]{0:T(1024)} %get-tuple-element.316) | copy-start | bytes 9220
  (55 other events, 810.6 us)
Sparse Core Ops, SparseCore 0:
  105.3 31.0 all-gather.6
  138.6 28.4 all-gather.4
  313.1 60.3 reduce-scatter.6
  500.2 60.3 reduce-scatter.8
  670.6 60.4 reduce-scatter.10
  990.1 37.8 reduce-scatter.12
  1030.5 37.7 reduce-scatter.14
  1076.0 60.4 reduce-scatter.16
Sparse Core Ops, SparseCore 1:
  377.8 24.3 all-gather.8
  403.9 23.8 all-gather.10
